TPU v7x, 128 devices: a whole 4x4x4 slice. The times are simulated.
128 devices in a mesh: seq: 4 (over x), tp: 32 (over z, y, core).
Axes of the slice: x: 4, y: 4, z: 4, core: 2. Of those that a mesh axis runs over, the one named last changes fastest.
Arguments:
- hidden_in: bfloat16 [96, 4, 1024], P('tp'), may hold values from -6 to 6
- new_query: bfloat16 [96, 4, 1024], P('tp'), may hold values from -70 to 70
- new_key: bfloat16 [96, 4, 1024], P('tp'), may hold values from -15 to 15
- new_value: bfloat16 [96, 4, 1024], P('tp'), may hold values from -6 to 6
- key_cache: bfloat16 [96, 4096, 1024], P('tp', 'seq'), may hold values from -16 to 16
- value_cache: bfloat16 [96, 4096, 1024], P('tp', 'seq'), may hold values from -6 to 6
- lengths: int32 [96], P('tp'), may hold values from 64 to 4096, as said below
- out_weight: bfloat16 [1024, 1024], replicated, may hold values from -0.1875 to 0.1875
- norm_gain: float32 [1024], replicated, may hold values from 0.5 to 1.5
- router_weight: bfloat16 [1024, 16], replicated, may hold values from -0.1875 to 0.1875
- expert_ids: int32 [96, 4, 2], P('tp'), may hold values from 0 to 15, all different within a row
- gate_weight: bfloat16 [45056, 1024], P(('seq', 'tp')), may hold values from -0.1875 to 0.1875
- up_weight: bfloat16 [45056, 1024], P(('seq', 'tp')), may hold values from -0.1875 to 0.1875
- down_weight: bfloat16 [45056, 1024], P(('seq', 'tp')), may hold values from -0.109375 to 0.109375
Outputs:
- attn_out: bfloat16 [96, 4, 1024], P('tp', None, 'seq')
- layer_out: bfloat16 [96, 4, 1024], P('tp', None, 'seq')
Inputs may be any that keep to these rules, and one draw needn't show every extreme that they name: `lengths`: each length is 4096 or between 64 and 128; some request has 4096.
All inputs are finite; a program needn't handle non-finite values.
Results may differ from a plain program's by a relative error of at most 0.014.
Values may be sent and summed in bfloat16 or wider, within the bound.
A program may use at most 64 MiB of HBM per device.

v0:
```python
import jax
import jax.numpy as jnp
from jax import lax
from jax.sharding import PartitionSpec as P

HEADS = 16
masked_score = -1e30
norm_epsilon = 1e-06


def entering(part, axis, combine, identity):
    place = lax.axis_index(axis)
    gathered = lax.all_gather(part, axis)
    state = jnp.zeros_like(part) + jnp.asarray(identity, part.dtype)

    def one(turn, state):
        return combine(state, lax.dynamic_index_in_dim(gathered, turn, 0, False))

    return lax.fori_loop(0, place, one, state)


def add_counts(former, latter):
    return former + latter


def pick_slot(chosen_ids, earlier):
    onehot = chosen_ids[..., None] == jnp.arange(earlier.shape[2], dtype=jnp.int32)
    return jnp.sum(jnp.where(onehot, earlier[:, :, None, :], 0), axis=3)


def body(
    hidden_in,
    new_query,
    new_key,
    new_value,
    key_cache,
    value_cache,
    lengths,
    out_weight,
    norm_gain,
    router_weight,
    expert_ids,
    gate_weight,
    up_weight,
    down_weight,
):
    req_dev, steps, width = hidden_in.shape
    block = key_cache.shape[1]
    head_size = width // HEADS
    scale = head_size ** (-0.5)
    seq_index = lax.axis_index("seq")
    tp_index = lax.axis_index("tp")
    seq_size = lax.axis_size("seq")
    tp_size = lax.axis_size("tp")
    queries = new_query.reshape(req_dev, steps, HEADS, head_size)
    cache_keys = key_cache.reshape(req_dev, block, HEADS, head_size)
    cache_values = value_cache.reshape(req_dev, block, HEADS, head_size)
    fresh_keys = new_key.reshape(req_dev, steps, HEADS, head_size)
    fresh_values = new_value.reshape(req_dev, steps, HEADS, head_size)
    scores = (
        jnp.einsum("rthe,rphe->rhtp", queries, cache_keys, preferred_element_type=jnp.float32)
        * scale
    )
    positions = seq_index * block + jnp.arange(block, dtype=jnp.int32)
    usable = (positions[None, :] < lengths[:, None])[:, None, None, :]
    scores = jnp.where(usable, scores, masked_score)
    fresh_scores = (
        jnp.einsum("rthe,rshe->rhts", queries, fresh_keys, preferred_element_type=jnp.float32)
        * scale
    )
    causal = (jnp.arange(steps)[:, None] >= jnp.arange(steps)[None, :]) & (seq_index == 0)
    fresh_scores = jnp.where(causal, fresh_scores, masked_score)
    local_max = jnp.maximum(jnp.max(scores, axis=3), jnp.max(fresh_scores, axis=3))
    weights = jnp.where(usable, jnp.exp(scores - local_max[..., None]), 0.0)
    fresh_weights = jnp.where(causal, jnp.exp(fresh_scores - local_max[..., None]), 0.0)
    totals = jnp.sum(weights, axis=3) + jnp.sum(fresh_weights, axis=3)
    gathered_values = jnp.einsum(
        "rhtp,rphe->rhte",
        weights.astype(jnp.bfloat16),
        cache_values,
        preferred_element_type=jnp.float32,
    )
    gathered_values = gathered_values + jnp.einsum(
        "rhts,rshe->rhte",
        fresh_weights.astype(jnp.bfloat16),
        fresh_values,
        preferred_element_type=jnp.float32,
    )
    overall = lax.pmax(local_max, "seq")
    factors = jnp.exp(local_max - overall)
    totals, gathered_values = (
        lax.psum((totals * factors).astype(jnp.bfloat16), "seq").astype(jnp.float32),
        lax.psum((gathered_values * factors[..., None]).astype(jnp.bfloat16), "seq").astype(
            jnp.float32
        ),
    )
    context = (
        (gathered_values / totals[..., None])
        .transpose(0, 2, 1, 3)
        .reshape(req_dev, steps, width)
        .astype(jnp.bfloat16)
    )
    attention = jnp.einsum("rtd,de->rte", context, out_weight, preferred_element_type=jnp.float32)
    feature_block = width // seq_size
    attn_out = lax.dynamic_slice_in_dim(
        attention, seq_index * feature_block, feature_block, 2
    ).astype(jnp.bfloat16)
    residual = hidden_in.astype(jnp.float32) + attention
    normed = (
        residual
        * lax.rsqrt(jnp.mean(residual * residual, axis=-1, keepdims=True) + norm_epsilon)
        * norm_gain
    ).astype(jnp.bfloat16)
    experts = router_weight.shape[1]
    topk = expert_ids.shape[2]
    requests = req_dev * tp_size
    capacity = (5 * requests * topk + 4 * experts - 1) // (4 * experts)
    expert_range = jnp.arange(experts, dtype=jnp.int32)
    local_hits = jnp.sum((expert_ids[..., None] == expert_range).astype(jnp.int32), axis=2)
    counts = jnp.sum(local_hits, axis=0)
    before = entering(counts, "tp", add_counts, jnp.zeros_like(counts))
    earlier = (before[None] + jnp.cumsum(local_hits, axis=0) - local_hits).astype(jnp.int32)
    routing = jnp.concatenate([expert_ids, pick_slot(expert_ids, earlier)], axis=2)
    all_routing = lax.all_gather(routing, "tp", axis=0, tiled=True)
    all_ids = all_routing[:, :, :topk]
    all_slots = all_routing[:, :, topk:]
    all_normed = lax.all_gather(normed, "tp", axis=0, tiled=True)
    logits = jnp.einsum(
        "rtd,de->rte", all_normed, router_weight, preferred_element_type=jnp.float32
    )
    onehot = all_ids[..., None] == expert_range
    chosen = jnp.sum(jnp.where(onehot, logits[:, :, None, :], 0.0), axis=3)
    share = 1.0 / (1.0 + jnp.exp(chosen[:, :, ::-1] - chosen))
    slices = seq_size * tp_size // experts
    mine = (seq_index * tp_size + tp_index) // slices
    match = all_ids == mine
    slot_mine = jnp.sum(jnp.where(match, all_slots, 0), axis=2)
    share_mine = jnp.sum(jnp.where(match, share, 0.0), axis=2)
    kept = jnp.any(match, axis=2) & (slot_mine < capacity)
    select = kept[None] & (slot_mine[None] == jnp.arange(capacity, dtype=jnp.int32)[:, None, None])
    buffer = (
        jnp.einsum(
            "crt,rtd->tcd",
            select.astype(jnp.bfloat16),
            all_normed,
            preferred_element_type=jnp.float32,
        )
        .astype(jnp.bfloat16)
        .reshape(steps * capacity, width)
    )
    contract = (((1,), (1,)), ((), ()))
    gate = lax.dot_general(buffer, gate_weight, contract, preferred_element_type=jnp.float32)
    upward = lax.dot_general(buffer, up_weight, contract, preferred_element_type=jnp.float32)
    inner = (jax.nn.gelu(gate) * upward).astype(jnp.bfloat16)
    produced = jnp.dot(inner, down_weight, preferred_element_type=jnp.float32)
    placed = select.astype(jnp.float32) * share_mine[None]
    term = jnp.einsum(
        "crt,tcd->rtd",
        placed,
        produced.reshape(steps, capacity, width),
        precision=lax.Precision.HIGHEST,
    )
    row_sums = lax.psum_scatter(term.astype(jnp.bfloat16), "tp", scatter_dimension=0, tiled=True)
    mixture = lax.psum_scatter(row_sums, "seq", scatter_dimension=2, tiled=True).astype(jnp.float32)
    own_residual = lax.dynamic_slice_in_dim(residual, seq_index * feature_block, feature_block, 2)
    layer_out = (own_residual + mixture).astype(jnp.bfloat16)
    return (attn_out, layer_out)


def solution(mesh):
    return jax.shard_map(
        body,
        mesh=mesh,
        in_specs=(
            P("tp", None, None),
            P("tp", None, None),
            P("tp", None, None),
            P("tp", None, None),
            P("tp", "seq", None),
            P("tp", "seq", None),
            P("tp"),
            P(),
            P(),
            P(),
            P("tp", None, None),
            P(("seq", "tp"), None),
            P(("seq", "tp"), None),
            P(("seq", "tp"), None),
        ),
        out_specs=(P("tp", None, "seq"), P("tp", None, "seq")),
        check_vma=False,
    )
```

profile of v0, /device:TPU:0, one launch (start us, length us, event | category | flops | bytes accessed | tf_op | source)
XLA Modules:
  0.0 284.9 jit_solution(4095929092177931425)
XLA Ops:
  7.2 0.0 copy-start
  7.2 0.0 all-reduce.4.cloned.1.call-start
  7.2 1.0 reshape.92
  8.2 0.0 copy-start.3
  8.2 0.0 copy-start.6
  8.2 8.7 %copy.131 = bf16[3,1024,1024]{1,2,0:T(8,128)(2,1)} copy(bf16[3,1024,1024]{2,1,0:T(8,128)(2,1)} %param.20) | data formatting | bytes 12582912 | tf_op args[4]
  16.9 0.0 copy-done.3
  16.9 0.1 reshape.94
  17.0 0.2 fusion.30
  17.2 0.1 copy.135
  17.3 0.1 fusion.43
  17.5 0.1 copy.136
  17.6 0.0 copy-done.6
  17.6 0.1 broadcast_compare_fusion
  17.6 3.8 %fusion.61 = (f32[3,16,4]{2,1,0:T(8,128)S(1)}, f32[3,16,4,1024]{3,2,1,0:T(4,128)S(1)}) fusion(bf16[3,1024,16,64]{1,3,2,0:T(8,128)(2,1)} %bitcast.35, bf16[3,4,16,64]{3,2,1,0:T(8,128)(2,1)S(1)} %reshape.92, pred[3,1024]{1,0:T(4,128)(4,1)S(1)} %broadcast_compare_fusion), kind=kOutput, calls=%fused_computation.93 | convolution fusion | flops 25755456 | bytes 7106304 | tf_op jit(solution)/shard_map/rthe,rphe->rhtp/dot_general | solution.py:61
  21.4 0.1 copy.138
  21.5 17.1 %pmax.7 = f32[3,16,4]{2,1,0:T(8,128)S(1)} all-reduce(f32[3,16,4]{2,1,0:T(8,128)S(1)} %max.9), channel_id=1, replica_groups=mesh['seq'=4,'tp'=32] {'seq'}, use_global_device_ids=true, to_apply=%region_2.3 | all-reduce | flops 192 | bytes 1536 | tf_op jit(solution)/shard_map/pmax | solution.py:89
  38.6 0.5 fusion.12
  39.1 0.1 fusion.50
  39.2 0.1 copy.141
  39.3 8.6 %copy.137 = bf16[3,1024,1024]{1,2,0:T(8,128)(2,1)} copy(bf16[3,1024,1024]{2,1,0:T(8,128)(2,1)} %param.21) | data formatting | bytes 12582912 | tf_op args[5]
  48.0 0.0 copy-start.7
  48.0 4.6 %fusion.14 = f32[3,16,4,64]{3,2,1,0:T(4,128)S(1)} fusion(bf16[3,1024,16,64]{1,3,2,0:T(8,128)(2,1)} %bitcast.36, f32[3,16,4,1024]{3,2,1,0:T(4,128)S(1)} %get-tuple-element.49, f32[3,16,4]{2,1,0:T(8,128)S(1)} %max.9, pred[3,1024]{1,0:T(4,128)(4,1)S(1)} %broadcast_compare_fusion), kind=kOutput, calls=%fused_computation.22 | convolution fusion | flops 25755648 | bytes 7130880 | tf_op jit(solution)/shard_map/rhtp,rphe->rhte/dot_general | solution.py:77
  52.6 0.2 copy.139
  52.8 0.0 copy-done.4
  52.8 0.1 reshape.96
  52.9 0.2 fusion.5
  53.1 14.9 %all-reduce.1 = (bf16[3,16,4,64]{3,2,1,0:T(4,128)(2,1)S(1)}, bf16[3,16,4]{2,1,0:T(8,128)(2,1)S(1)}) all-reduce(bf16[3,16,4,64]{3,2,1,0:T(4,128)(2,1)S(1)} %fusion.5, bf16[3,16,4]{2,1,0:T(8,128)(2,1)S(1)} %get-tuple-element.42), channel_id=1, replica_groups=mesh['seq'=4,'tp'=32] {'seq'}, use_global_device_ids=true, to_apply=%region_3.4 | all-reduce | flops 12480 | bytes 49920 | tf_op jit(solution)/shard_map/psum | solution.py:93
  68.0 0.1 fusion.28
  68.2 0.1 convert_element_type.67
  68.3 0.0 copy-done
  68.3 0.0 copy-done.2
  68.3 0.5 multiply_reduce_fusion
  68.8 0.0 copy-done.5
  68.8 0.1 multiply_convert_fusion
  68.9 26.4 %all_gather.15 = bf16[96,4,1024]{2,1,0:T(4,128)(2,1)S(1)} all-gather(bf16[3,4,1024]{2,1,0:T(4,128)(2,1)S(1)} %multiply_convert_fusion), channel_id=1, replica_groups=mesh['seq'=4,'tp'=32] {'tp'}, dimensions={0}, use_global_device_ids=true | all-gather | bytes 811008 | tf_op jit(solution)/shard_map/all_gather | solution.py:127
  95.3 0.1 convert_reduce_fusion.1
  95.3 23.6 %all-gather.1 = s32[32,4,16]{2,1,0:T(4,128)S(1)} all-gather(s32[1,4,16]{2,1,0:T(4,128)S(1)} %bitcast.39), channel_id=2, replica_groups=mesh['seq'=4,'tp'=32] {'tp'}, dimensions={0}, use_global_device_ids=true | all-gather | bytes 8448 | tf_op jit(solution)/shard_map/all_gather | solution.py:13
  119.0 0.3 select_reduce_fusion.1
  119.2 0.1 copy.143
  119.3 23.6 %all_gather.14 = s32[96,4,4]{2,1,0:T(4,128)S(1)} all-gather(s32[3,4,4]{2,1,0:T(4,128)S(1)} %copy.143), channel_id=1, replica_groups=mesh['seq'=4,'tp'=32] {'tp'}, dimensions={0}, use_global_device_ids=true | all-gather | bytes 6336 | tf_op jit(solution)/shard_map/all_gather | solution.py:124
  142.9 0.2 fusion.60
  143.1 0.1 copy.161
  143.2 0.4 fusion.9
  143.7 0.1 copy.162
  143.8 0.1 fusion.52
  143.9 0.5 convolution_convert_fusion.1
  144.5 1.5 fusion.62
  145.9 2.0 fusion.7
  148.0 1.4 fusion.2
  149.4 1.5 copy.155
  150.9 0.0 all-reduce.4.cloned.1.call-update
  150.9 0.0 reduce-scatter.4.cloned.1.call-start
  151.0 0.6 dynamic-slice
  152.2 101.1 %all-reduce.4.cloned.1.call-done = bf16[96,4,1024]{2,1,0:T(4,128)(2,1)} async-done(((bf16[96,4,1024]{2,1,0:T(4,128)(2,1)}), bf16[96,4,1024]{2,1,0:T(4,128)(2,1)}) %all-reduce.4.cloned.1.call-update) | async-done | bytes 786448
  253.3 0.7 constant_dynamic-slice_fusion
  254.1 0.7 copy.156
  254.8 1.2 reshape.105
  256.0 0.0 reduce-scatter.4.cloned.1.call-update
  256.0 0.6 dynamic-slice_convert_fusion
  256.6 19.6 %reduce-scatter.4.cloned.1.call-done = bf16[256,12]{1,0:T(8,128)(2,1)} async-done(((bf16[1024,12]{1,0:T(8,128)(2,1)}), bf16[256,12]{1,0:T(8,128)(2,1)}) %reduce-scatter.4.cloned.1.call-update) | async-done | bytes 6160
  276.3 1.0 reshape.106
  277.2 0.2 copy.157
  277.4 0.6 add_convert_fusion
  (26 shorter events, 0.3 us)
Async XLA Ops:
  7.2 61.1 %copy-start = (bf16[1024,1024]{1,0:T(8,128)(2,1)S(1)}, bf16[1024,1024]{1,0:T(8,128)(2,1)}, u32[]{:S(2)}) copy-start(bf16[1024,1024]{1,0:T(8,128)(2,1)} %param.23) | copy-start | bytes 6291460
  7.2 246.2 %all-reduce.4.cloned.1.call-start = ((), (), s32[]{:S(2)}) async-start(), calls=%async_computation.2 | async-start | bytes 1572864
  8.2 8.7 %copy-start.3 = (bf16[3,4,1024]{2,1,0:T(4,128)(2,1)S(1)}, bf16[3,4,1024]{2,1,0:T(4,128)(2,1)}, u32[]{:S(2)}) copy-start(bf16[3,4,1024]{2,1,0:T(4,128)(2,1)} %param.18) | copy-start | bytes 73732
  8.2 9.3 %copy-start.6 = (s32[3]{0:T(128)S(1)}, s32[3]{0:T(128)}, u32[]{:S(2)}) copy-start(s32[3]{0:T(128)} %param.22) | copy-start | bytes 40
  48.0 4.8 %copy-start.4 = (bf16[3,4,1024]{2,1,0:T(4,128)(2,1)S(1)}, bf16[3,4,1024]{2,1,0:T(4,128)(2,1)}, u32[]{:S(2)}) copy-start(bf16[3,4,1024]{2,1,0:T(4,128)(2,1)} %param.19) | copy-start | bytes 73732
  48.0 20.3 %copy-start.2 = (bf16[3,4,1024]{2,1,0:T(4,128)(2,1)S(1)}, bf16[3,4,1024]{2,1,0:T(4,128)(2,1)}, u32[]{:S(2)}) copy-start(bf16[3,4,1024]{2,1,0:T(4,128)(2,1)} %param.16) | copy-start | bytes 73732
  48.0 20.8 %copy-start.5 = (f32[1024]{0:T(1024)S(1)}, f32[1024]{0:T(1024)}, u32[]{:S(2)}) copy-start(f32[1024]{0:T(1024)} %param.24) | copy-start | bytes 12292
  48.0 47.3 %copy-start.1 = (s32[3,4,2]{1,2,0:T(2,128)S(1)}, s32[3,4,2]{1,2,0:T(2,128)}, u32[]{:S(2)}) copy-start(s32[3,4,2]{1,2,0:T(2,128)} %param.26) | copy-start | bytes 292
  48.0 95.2 %copy-start.7 = (bf16[1024,16]{0,1:T(8,128)(2,1)S(1)}, bf16[1024,16]{0,1:T(8,128)(2,1)}, u32[]{:S(2)}) copy-start(bf16[1024,16]{0,1:T(8,128)(2,1)} %param.25) | copy-start | bytes 98308
  68.8 82.2 %copy-start.8 = (u32[128]{0:T(128)S(1)}, u32[128]{0:T(128)}, u32[]{:S(2)}) copy-start(u32[128]{0:T(128)} %constant.85) | copy-start | bytes 1540
  150.9 125.3 %reduce-scatter.4.cloned.1.call-start = ((), (), s32[]{:S(2)}) async-start(), calls=%async_computation.1 | async-start | bytes 327680
Sparse Core Ops, SparseCore 0:
  151.1 102.2 all-reduce.3
  256.1 20.0 reduce-scatter.3
where the time goes:
time: 286 us; the launch traced here: 285 us
  waiting for transfers between devices  121 us (42%)
  blocking collectives  106 us (37%)
  local copies, waits for them, and re-layouts  26.3 us (9%)
  matrix products  15.1 us (5%)
  between operations  15 us (5%)
    unnamed x4, waiting for transfers between devices  121 us
    all_gather x1, blocking collectives, body(): all_normed = lax.all_gather(normed, 'tp', axis=0, tiled=True)  26.4 us
    all_gather x1, blocking collectives, entering(): gathered = lax.all_gather(part, axis)  23.6 us
    all_gather x1, blocking collectives, body(): all_routing = lax.all_gather(routing, 'tp', axis=0, tiled=True)  23.6 us
    unnamed x28, local copies, waits for them, and re-layouts  21.9 us
    pmax x1, blocking collectives, body(): overall = lax.pmax(local_max, 'seq')  17.1 us
    psum x1, blocking collectives, body(): lax.psum((gathered_values * factors[..., None]).astype(jnp.bfloat16), 'seq')  14.9 us
  transfers between devices with their start and end apart: 2, of which 2 were waited for; matrix products, arithmetic and copies ran while one was open for 0% of the time, Pallas kernels for 0%

commit v1 on v0

--- a/solution.py
+++ b/solution.py
@@ -121,7 +121,8 @@
     before = entering(counts, "tp", add_counts, jnp.zeros_like(counts))
     earlier = (before[None] + jnp.cumsum(local_hits, axis=0) - local_hits).astype(jnp.int32)
     routing = jnp.concatenate([expert_ids, pick_slot(expert_ids, earlier)], axis=2)
-    all_routing = lax.all_gather(routing, "tp", axis=0, tiled=True)
+    stack = jnp.stack([routing] * lax.axis_size("tp"))
+    all_routing = jnp.concatenate(lax.all_to_all(stack, "tp", 0, 0), axis=0)
     all_ids = all_routing[:, :, :topk]
     all_slots = all_routing[:, :, topk:]
     all_normed = lax.all_gather(normed, "tp", axis=0, tiled=True)

time: 286 us -> 274 us (0.958)
  blocking collectives: 106 us -> 83 us
  starting transfers between devices: 0.08 us -> 6.29 us
  other arithmetic: 2.15 us -> 5.13 us
    all_gather x1 -> x0, blocking collectives: 23.6 us -> none  [body(): all_routing = lax.all_gather(routing, 'tp', axis=0, tiled=True)]
    all_to_all x0 -> x1, starting transfers between devices: none -> 6.2 us  [body(): all_routing = jnp.concatenate(lax.all_to_all(stack, 'tp', 0, 0), axis=0)]
    unnamed x28 -> x26, local copies, waits for them, and re-layouts: 21.9 us -> 21.9 us
  transfers between devices with their start and end apart: 2 -> 3, of which waited for: 2 -> 2; matrix products, arithmetic and copies ran while one was open for 0% -> 12% of each run, Pallas kernels for 0% -> 0%
where the time goes in v1:
time: 274 us; the launch traced here: 273 us
  waiting for transfers between devices  121 us (44%)
  blocking collectives  83 us (30%)
  local copies, waits for them, and re-layouts  26.9 us (10%)
  matrix products  15.7 us (6%)
  between operations  15 us (5%)
  starting transfers between devices  6.29 us (2%)
  other arithmetic  5.13 us (2%)
    unnamed x4, waiting for transfers between devices  121 us
    all_gather x1, blocking collectives, entering(): gathered = lax.all_gather(part, axis)  25.7 us
    all_gather x1, blocking collectives, body(): all_normed = lax.all_gather(normed, 'tp', axis=0, tiled=True)  25.4 us
    unnamed x26, local copies, waits for them, and re-layouts  21.9 us
    pmax x1, blocking collectives, body(): overall = lax.pmax(local_max, 'seq')  17 us
    psum x1, blocking collectives, body(): lax.psum((gathered_values * factors[..., None]).astype(jnp.bfloat16), 'seq')  14.9 us
    all_to_all x1, starting transfers between devices, body(): all_routing = jnp.concatenate(lax.all_to_all(stack, 'tp', 0, 0), axis=0)  6.2 us
  transfers between devices with their start and end apart: 3, of which 2 were waited for; matrix products, arithmetic and copies ran while one was open for 12% of the time, Pallas kernels for 0%

profile of v1, /device:TPU:0, one launch (start us, length us, event | category | flops | bytes accessed | tf_op | source)
XLA Modules:
  0.0 272.6 jit_solution(218410968666054528)
XLA Ops:
  7.2 0.0 copy-start
  7.2 0.9 convert_reduce_fusion.1
  8.1 25.7 %all-gather.1 = s32[32,4,16]{2,1,0:T(4,128)S(1)} all-gather(s32[1,4,16]{2,1,0:T(4,128)S(1)} %bitcast.41), channel_id=2, replica_groups=mesh['seq'=4,'tp'=32] {'tp'}, dimensions={0}, use_global_device_ids=true | all-gather | bytes 8448 | tf_op jit(solution)/shard_map/all_gather | solution.py:13
  33.9 0.9 select_reduce_fusion.1
  34.8 0.7 pad_add_fusion
  35.5 0.1 copy.153
  35.6 0.7 stack.2
  36.3 6.2 %all-to-all-start = ((s32[32,3,4,4]{3,2,1,0:T(4,128)}), s32[32,3,4,4]{3,2,1,0:T(4,128)S(1)}, u32[]{:S(2)}, u32[]{:S(2)}) async-start(s32[32,3,4,4]{3,2,1,0:T(4,128)} %stack.2), calls=%async_computation | async-start | bytes 393216 | tf_op jit(solution)/shard_map/all_to_all | solution.py:125
  42.5 0.0 all-reduce.4.cloned.1.call-start
  42.6 0.8 reshape.97
  43.4 0.0 copy-start.2
  43.4 0.0 copy-start.5
  43.5 8.7 %copy.141 = bf16[3,1024,1024]{1,2,0:T(8,128)(2,1)} copy(bf16[3,1024,1024]{2,1,0:T(8,128)(2,1)} %param.20) | data formatting | bytes 12582912 | tf_op args[4]
  52.1 0.0 copy-done.2
  52.1 0.1 reshape.99
  52.2 0.2 fusion.30
  52.4 0.1 copy.145
  52.5 0.1 fusion.43
  52.7 0.1 copy.146
  52.8 0.1 broadcast_compare_fusion
  52.8 3.8 %fusion.61 = (f32[3,16,4]{2,1,0:T(8,128)S(1)}, f32[3,16,4,1024]{3,2,1,0:T(4,128)S(1)}) fusion(bf16[3,1024,16,64]{1,3,2,0:T(8,128)(2,1)} %bitcast.36, bf16[3,4,16,64]{3,2,1,0:T(8,128)(2,1)S(1)} %reshape.97, pred[3,1024]{1,0:T(4,128)(4,1)S(1)} %broadcast_compare_fusion), kind=kOutput, calls=%fused_computation.93 | convolution fusion | flops 25755456 | bytes 7106304 | tf_op jit(solution)/shard_map/rthe,rphe->rhtp/dot_general | solution.py:61
  56.6 0.1 copy.148
  56.7 17.0 %pmax.7 = f32[3,16,4]{2,1,0:T(8,128)S(1)} all-reduce(f32[3,16,4]{2,1,0:T(8,128)S(1)} %max.9), channel_id=1, replica_groups=mesh['seq'=4,'tp'=32] {'seq'}, use_global_device_ids=true, to_apply=%region_2.3 | all-reduce | flops 192 | bytes 1536 | tf_op jit(solution)/shard_map/pmax | solution.py:89
  73.8 0.5 fusion.12
  74.2 0.1 fusion.50
  74.3 0.1 copy.151
  74.4 8.6 %copy.147 = bf16[3,1024,1024]{1,2,0:T(8,128)(2,1)} copy(bf16[3,1024,1024]{2,1,0:T(8,128)(2,1)} %param.21) | data formatting | bytes 12582912 | tf_op args[5]
  83.1 4.6 %fusion.14 = f32[3,16,4,64]{3,2,1,0:T(4,128)S(1)} fusion(bf16[3,1024,16,64]{1,3,2,0:T(8,128)(2,1)} %bitcast.37, f32[3,16,4,1024]{3,2,1,0:T(4,128)S(1)} %get-tuple-element.49, f32[3,16,4]{2,1,0:T(8,128)S(1)} %max.9, pred[3,1024]{1,0:T(4,128)(4,1)S(1)} %broadcast_compare_fusion), kind=kOutput, calls=%fused_computation.22 | convolution fusion | flops 25755648 | bytes 7130880 | tf_op jit(solution)/shard_map/rhtp,rphe->rhte/dot_general | solution.py:77
  87.7 0.2 copy.149
  87.9 0.1 reshape.101
  88.0 0.2 fusion.5
  88.2 14.9 %all-reduce.1 = (bf16[3,16,4,64]{3,2,1,0:T(4,128)(2,1)S(1)}, bf16[3,16,4]{2,1,0:T(8,128)(2,1)S(1)}) all-reduce(bf16[3,16,4,64]{3,2,1,0:T(4,128)(2,1)S(1)} %fusion.5, bf16[3,16,4]{2,1,0:T(8,128)(2,1)S(1)} %get-tuple-element.42), channel_id=1, replica_groups=mesh['seq'=4,'tp'=32] {'seq'}, use_global_device_ids=true, to_apply=%region_3.4 | all-reduce | flops 12480 | bytes 49920 | tf_op jit(solution)/shard_map/psum | solution.py:93
  103.1 0.1 fusion.28
  103.3 0.1 convert_element_type.67
  103.4 0.0 copy-done
  103.4 0.0 copy-start.7
  103.4 0.5 multiply_reduce_fusion
  103.9 0.1 multiply_convert_fusion
  104.0 25.4 %all_gather.11 = bf16[96,4,1024]{2,1,0:T(4,128)(2,1)S(1)} all-gather(bf16[3,4,1024]{2,1,0:T(4,128)(2,1)S(1)} %multiply_convert_fusion), channel_id=1, replica_groups=mesh['seq'=4,'tp'=32] {'tp'}, dimensions={0}, use_global_device_ids=true | all-gather | bytes 811008 | tf_op jit(solution)/shard_map/all_gather | solution.py:128
  129.4 1.0 fusion.9
  130.4 0.0 all-to-all-done
  130.4 0.2 fusion.60
  130.5 0.1 copy.167
  130.6 0.8 select_reduce_fusion
  131.5 0.1 copy.168
  131.6 0.1 fusion.52
  131.7 0.5 convolution_convert_fusion.1
  132.3 1.5 fusion.62
  133.7 2.0 fusion.7
  135.8 1.4 fusion.2
  137.2 1.5 copy.160
  138.7 0.0 all-reduce.4.cloned.1.call-update
  138.8 0.0 reduce-scatter.4.cloned.1.call-start
  138.8 0.6 dynamic-slice
  140.1 101.0 %all-reduce.4.cloned.1.call-done = bf16[96,4,1024]{2,1,0:T(4,128)(2,1)} async-done(((bf16[96,4,1024]{2,1,0:T(4,128)(2,1)}), bf16[96,4,1024]{2,1,0:T(4,128)(2,1)}) %all-reduce.4.cloned.1.call-update) | async-done | bytes 786448
  241.1 0.7 constant_dynamic-slice_fusion
  241.8 0.7 copy.162
  242.6 1.2 reshape.111
  243.8 0.0 reduce-scatter.4.cloned.1.call-update
  243.8 0.6 dynamic-slice_convert_fusion
  244.4 19.6 %reduce-scatter.4.cloned.1.call-done = bf16[256,12]{1,0:T(8,128)(2,1)} async-done(((bf16[1024,12]{1,0:T(8,128)(2,1)}), bf16[256,12]{1,0:T(8,128)(2,1)}) %reduce-scatter.4.cloned.1.call-update) | async-done | bytes 6160
  264.0 1.0 reshape.112
  265.0 0.2 copy.163
  265.2 0.6 add_convert_fusion
  (26 shorter events, 0.2 us)
Async XLA Ops:
  7.2 96.2 %copy-start = (bf16[1024,1024]{1,0:T(8,128)(2,1)S(1)}, bf16[1024,1024]{1,0:T(8,128)(2,1)}, u32[]{:S(2)}) copy-start(bf16[1024,1024]{1,0:T(8,128)(2,1)} %param.23) | copy-start | bytes 6291460
  36.3 94.1 %all-to-all-start = ((s32[32,3,4,4]{3,2,1,0:T(4,128)}), s32[32,3,4,4]{3,2,1,0:T(4,128)S(1)}, u32[]{:S(2)}, u32[]{:S(2)}) async-start(s32[32,3,4,4]{3,2,1,0:T(4,128)} %stack.2), calls=%async_computation | async-start | bytes 393216 | tf_op jit(solution)/shard_map/all_to_all | solution.py:125
  42.5 198.6 %all-reduce.4.cloned.1.call-start = ((), (), s32[]{:S(2)}) async-start(), calls=%async_computation.3 | async-start | bytes 1572864
  43.4 8.7 %copy-start.2 = (bf16[3,4,1024]{2,1,0:T(4,128)(2,1)S(1)}, bf16[3,4,1024]{2,1,0:T(4,128)(2,1)}, u32[]{:S(2)}) copy-start(bf16[3,4,1024]{2,1,0:T(4,128)(2,1)} %param.18) | copy-start | bytes 73732
  43.4 9.3 %copy-start.5 = (s32[3]{0:T(128)S(1)}, s32[3]{0:T(128)}, u32[]{:S(2)}) copy-start(s32[3]{0:T(128)} %param.22) | copy-start | bytes 40
  83.1 4.8 %copy-start.3 = (bf16[3,4,1024]{2,1,0:T(4,128)(2,1)S(1)}, bf16[3,4,1024]{2,1,0:T(4,128)(2,1)}, u32[]{:S(2)}) copy-start(bf16[3,4,1024]{2,1,0:T(4,128)(2,1)} %param.19) | copy-start | bytes 73732
  83.1 20.3 %copy-start.1 = (bf16[3,4,1024]{2,1,0:T(4,128)(2,1)S(1)}, bf16[3,4,1024]{2,1,0:T(4,128)(2,1)}, u32[]{:S(2)}) copy-start(bf16[3,4,1024]{2,1,0:T(4,128)(2,1)} %param.16) | copy-start | bytes 73732
  83.1 20.8 %copy-start.4 = (f32[1024]{0:T(1024)S(1)}, f32[1024]{0:T(1024)}, u32[]{:S(2)}) copy-start(f32[1024]{0:T(1024)} %param.24) | copy-start | bytes 12292
  83.1 46.3 %copy-start.6 = (bf16[1024,16]{0,1:T(8,128)(2,1)S(1)}, bf16[1024,16]{0,1:T(8,128)(2,1)}, u32[]{:S(2)}) copy-start(bf16[1024,16]{0,1:T(8,128)(2,1)} %param.25) | copy-start | bytes 98308
  103.4 35.4 %copy-start.7 = (u32[128]{0:T(128)S(1)}, u32[128]{0:T(128)}, u32[]{:S(2)}) copy-start(u32[128]{0:T(128)} %constant.85) | copy-start | bytes 1540
  138.8 125.3 %reduce-scatter.4.cloned.1.call-start = ((), (), s32[]{:S(2)}) async-start(), calls=%async_computation.2 | async-start | bytes 327680
Sparse Core Ops, SparseCore 0:
  138.9 102.1 all-reduce.3
  243.9 20.0 reduce-scatter.3
